TPU v7x, 32 devices: a whole 2x2x4 slice. The times are simulated.
32 devices in a mesh: groups: 1, replica: 32 (over z, y, x, core).
Axes of the slice: x: 2, y: 2, z: 4, core: 2. Of those that a mesh axis runs over, the one named last changes fastest.
Arguments:
- queries: bfloat16 [8192, 1024], P(('groups', 'replica')), may hold values from -15 to 15
- suffix_kv: bfloat16 [8192, 256], P(('groups', 'replica')), may hold values from -6 to 6
- own_cache: bfloat16 [16384, 256], P(('groups', 'replica')), may hold values from -6 to 6
- ctx_len: int32 [32], P(('groups', 'replica')), may hold values from 64 to 512, as said below
- prefix_cache: bfloat16 [131072, 256], P(('groups', 'replica')), may hold values from -18 to 18
- owners: int32 [2], P('groups'), may hold values from 0 to 31, as said below
- readers: int32 [32], P('groups'), may hold values from 0 to 1
- kv_pool: bfloat16 [1024, 128, 256], P(('groups', 'replica')), may hold values from -6 to 6
- mig_target: int32 [32, 32], P(('groups', 'replica')), may hold values from 0 to 31, as said below
- mig_block: int32 [32, 32], P(('groups', 'replica')), may hold values from 0 to 31, each once within a row
- mig_count: int32 [32], P(('groups', 'replica')), may hold values from 8 to 32, as said below
Outputs:
- attended: bfloat16 [8192, 1024], P(('groups', 'replica'))
Inputs may be any that keep to these rules, and one draw needn't show every extreme that they name: `owners`: 2 different replicas; replica 32 - 1 owns one prefix in every draw. `ctx_len`: the largest value is 512 in every draw. `mig_target`: each row names every replica once, so one source sends at most one block to one target; in every draw one replica is the first entry of every row. `mig_block`: each row names every block of the source's pool once. `mig_count`: the largest value is 32 in every draw.
All inputs are finite; a program needn't handle non-finite values.
Results may differ from a plain program's by a relative error of at most 0.0019.
Values may be sent and summed in bfloat16 or wider, within the bound.
A program may use at most 128 MiB of HBM per device.

v0:
```python
import jax
import jax.numpy as jnp
from jax import lax
from jax.sharding import PartitionSpec as P


def fold_block(carried, query_rows, key_value, allowed):
    running_max, denominator, numerator = carried
    head_size = key_value.shape[1] // 2
    scores = lax.dot_general(
        query_rows,
        key_value[:, :head_size],
        (((1,), (1,)), ((), ())),
        preferred_element_type=jnp.float32,
    ) * head_size ** (-0.5)
    scores = jnp.where(allowed, scores, -jnp.inf)
    new_max = jnp.maximum(running_max, jnp.max(scores, axis=1))
    shrink = jnp.exp(running_max - new_max)
    weights = jnp.exp(scores - new_max[:, None])
    denominator = denominator * shrink + jnp.sum(weights, axis=1)
    numerator = numerator * shrink[:, None] + jnp.dot(
        weights.astype(jnp.bfloat16), key_value[:, head_size:], preferred_element_type=jnp.float32
    )
    return (new_max, denominator, numerator)


def fold_keys(carried, query_rows, key_value, key_mask):
    key_count = key_value.shape[0]
    if key_count > 1024 and key_count % 1024 == 0:
        blocks = key_value.reshape(key_count // 1024, 1024, key_value.shape[1])
        mask_rows = key_mask.reshape(key_count // 1024, 1024)

        def step_block(partial_value, block_pair):
            return (
                fold_block(partial_value, query_rows, block_pair[0], block_pair[1][None, :]),
                None,
            )

        carried, unused = lax.scan(step_block, carried, (blocks, mask_rows))
        return carried
    return fold_block(carried, query_rows, key_value, key_mask[None, :])


def on_device(
    queries,
    suffix_kv,
    own_cache,
    ctx_len,
    prefix_cache,
    owners,
    readers,
    kv_pool,
    mig_target,
    mig_block,
    mig_count,
):
    replicas = lax.axis_size("replica")
    head_size = suffix_kv.shape[1] // 2
    head_count = queries.shape[1] // head_size
    query_rows = queries.reshape(-1, head_size)
    row_count = query_rows.shape[0]
    suffix_len = suffix_kv.shape[0]
    carried = (
        jnp.full((row_count,), -jnp.inf, jnp.float32),
        jnp.zeros((row_count,), jnp.float32),
        jnp.zeros((row_count, head_size), jnp.float32),
    )
    targets = mig_target[0]
    block_ids = mig_block[0]
    entry_live = jnp.arange(targets.shape[0], dtype=jnp.int32) < mig_count[0]
    matching = (targets[None, :] == jnp.arange(replicas, dtype=jnp.int32)[:, None]) & entry_live[
        None, :
    ]
    slot_ids = jnp.sum(jnp.where(matching, block_ids[None, :], 0), axis=1)
    slot_flags = jnp.any(matching, axis=1).astype(jnp.bfloat16)
    outgoing = kv_pool[slot_ids]
    arrived, arrived_flags = (
        lax.all_to_all(outgoing, "replica", split_axis=0, concat_axis=0, tiled=True),
        lax.all_to_all(slot_flags, "replica", split_axis=0, concat_axis=0, tiled=True),
    )
    pieces = prefix_cache.reshape(replicas, -1, prefix_cache.shape[1])
    spread = lax.all_to_all(pieces, "replica", split_axis=0, concat_axis=0, tiled=True)
    held = spread[owners]
    outgoing_pieces = held[readers]
    collected = lax.all_to_all(outgoing_pieces, "replica", split_axis=0, concat_axis=0, tiled=True)
    shared = collected.reshape(prefix_cache.shape)
    positions = jnp.arange(row_count, dtype=jnp.int32) // head_count
    causal = jnp.arange(suffix_len, dtype=jnp.int32)[None, :] <= positions[:, None]
    carried = fold_block(carried, query_rows, suffix_kv, causal)
    own_mask = jnp.arange(own_cache.shape[0], dtype=jnp.int32) < ctx_len[0]
    carried = fold_keys(carried, query_rows, own_cache, own_mask)
    moved_rows = arrived.reshape(-1, arrived.shape[2])
    moved_mask = jnp.repeat(arrived_flags > 0, arrived.shape[1])
    carried = fold_keys(carried, query_rows, moved_rows, moved_mask)
    carried = fold_keys(carried, query_rows, shared, jnp.ones((shared.shape[0],), bool))
    running_max, denominator, numerator = carried
    return (numerator / denominator[:, None]).astype(jnp.bfloat16).reshape(queries.shape)


def solution(mesh):
    in_specs = (
        P(("groups", "replica"), None),
        P(("groups", "replica"), None),
        P(("groups", "replica"), None),
        P(("groups", "replica")),
        P(("groups", "replica"), None),
        P("groups"),
        P("groups"),
        P(("groups", "replica"), None, None),
        P(("groups", "replica"), None),
        P(("groups", "replica"), None),
        P(("groups", "replica")),
    )
    out_specs = P(("groups", "replica"), None)
    return jax.shard_map(
        on_device, mesh=mesh, in_specs=in_specs, out_specs=out_specs, check_vma=False
    )
```

profile of v0, /device:TPU:0, one launch (start us, length us, event | category | flops | bytes accessed | tf_op | source)
XLA Modules:
  0.0 203.9 jit_solution(16879425851371043175)
XLA Ops:
  1.7 14.3 %all_to_all.21 = bf16[32,1,1]{2,1,0:T(2,128)(2,1)S(1)} all-to-all(bf16[32,1,1]{2,1,0:T(2,128)(2,1)S(1)} %copy.14), channel_id=1, replica_groups=mesh['groups'=1,'replica'=32] {'replica'}, dimensions={0} | all-to-all | bytes 128 | tf_op jit(solution)/shard_map/all_to_all | solution.py:79
  16.0 3.5 %all-to-all-start.2 = ((bf16[32,128,256]{2,1,0:T(8,128)(2,1)}), bf16[32,128,256]{2,1,0:T(8,128)(2,1)}, u32[]{:S(2)}, u32[]{:S(2)}) async-start(bf16[32,128,256]{2,1,0:T(8,128)(2,1)} %bitcast.36), calls=%async_computation.2 | async-start | bytes 4194304 | tf_op jit(solution)/shard_map/all_to_all | solution.py:82
  19.7 2.0 gather_fusion
  21.8 46.6 %all-to-all-done.2 = bf16[32,128,256]{2,1,0:T(8,128)(2,1)} async-done(((bf16[32,128,256]{2,1,0:T(8,128)(2,1)}), bf16[32,128,256]{2,1,0:T(8,128)(2,1)}, u32[]{:S(2)}, u32[]{:S(2)}) %all-to-all-start.2) | async-done | bytes 2097184 | tf_op jit(solution)/shard_map/all_to_all | solution.py:82
  68.3 4.1 %all-to-all-start.1 = ((bf16[32,128,256]{2,1,0:T(8,128)(2,1)}), bf16[32,128,256]{2,1,0:T(8,128)(2,1)}, u32[]{:S(2)}, u32[]{:S(2)}) async-start(bf16[32,128,256]{2,1,0:T(8,128)(2,1)} %gather_fusion), calls=%async_computation.1 | async-start | bytes 4194304 | tf_op jit(solution)/shard_map/all_to_all | solution.py:78
  76.8 2.3 %convolution_add_fusion = f32[2048,128]{1,0:T(8,128)} fusion(f32[2048,128]{1,0:T(8,128)S(1)} %fusion.31, f32[2048,512]{0,1:T(8,128)S(1)} %get-tuple-element.122, f32[2048]{0:T(1024)S(1)} %max.16, pred[512]{0:T(512)(128)(4,1)S(1)} %iota_compare_fusion.2, bf16[512,256]{1,0:T(8,128)(2,1)S(1)} %copy-done.6), kind=kOutput, calls=%fused_computation.42 | convolution fusion | flops 272891904 | bytes 6431232 | tf_op jit(solution)/shard_map/dot_general | solution.py:21
  80.0 2.1 %gather_fusion.1 = bf16[2,128,256]{2,1,0:T(8,128)(2,1)S(1)} fusion(bf16[32,128,256]{2,1,0:T(8,128)(2,1)} %all-to-all-done.2, s32[1024]{0:T(1024)S(1)} %pad_clamp_fusion.1), kind=kCustom, calls=%fused_computation.1 | custom fusion | bytes 262152 | tf_op jit(solution)/shard_map/gather | solution.py:83
  82.1 2.0 gather_fusion.2
  84.1 37.0 %all-to-all-done.1 = bf16[32,128,256]{2,1,0:T(8,128)(2,1)} async-done(((bf16[32,128,256]{2,1,0:T(8,128)(2,1)}), bf16[32,128,256]{2,1,0:T(8,128)(2,1)}, u32[]{:S(2)}, u32[]{:S(2)}) %all-to-all-start.1) | async-done | bytes 2097184 | tf_op jit(solution)/shard_map/all_to_all | solution.py:78
  121.1 4.4 %all-to-all-start.3 = ((bf16[32,128,256]{2,1,0:T(8,128)(2,1)}), bf16[32,128,256]{2,1,0:T(8,128)(2,1)}, u32[]{:S(2)}, u32[]{:S(2)}) async-start(bf16[32,128,256]{2,1,0:T(8,128)(2,1)} %gather_fusion.2), calls=%async_computation.3 | async-start | bytes 4194304 | tf_op jit(solution)/shard_map/all_to_all | solution.py:85
  125.5 34.7 %while.28 = (s32[]{:T(128)}, f32[2048]{0:T(1024)S(1)}, f32[2048]{0:T(1024)S(1)}, f32[2048,128]{1,0:T(8,128)}, pred[4,1024]{1,0:T(4,128)(4,1)S(1)}, /*index=5*/bf...) while((s32[]{:T(128)}, f32[2048]{0:T(1024)S(1)}, f32[2048]{0:T(1024)S(1)}, ...), condition=%wide.region_9.10_spmd, body=%wide.region_6.9_spmd.sunk | while | flops 1097338880 | bytes 37885076 | solution.py:39
  126.7 1.6 fusion.72
  128.3 2.5 %fusion.73 = f32[2048]{0:T(1024)S(1)} fusion(f32[1024,2048]{1,0:T(8,128)S(1)} %get-tuple-element.206, f32[2048]{0:T(1024)S(1)} %max.19, pred[1024]{0:T(1024)(128)(4,1)S(1)} %dynamic-slice_reduce_fusion.2), kind=kLoop, calls=%fused_computation.22.clone.1 | loop fusion | flops 8386560 | bytes 8406016 | tf_op jit(solution)/shard_map/while/body/eval_jaxpr/reduce_sum | solution.py:20
  130.8 2.5 %fusion.74 = f32[2048,128]{1,0:T(8,128)S(1)} fusion(f32[1024,2048]{1,0:T(8,128)S(1)} %get-tuple-element.206, f32[2048]{0:T(1024)S(1)} %max.19, pred[1024]{0:T(1024)(128)(4,1)S(1)} %dynamic-slice_reduce_fusion.2, f32[2048,128]{1,0:T(8,128)S(1)} %copy-done.1, f32[2048]{0:T(1024)S(1)} %get-tuple-element.208, ...), kind=kOutput, calls=%fused_computation.25.clone.1 | convolution fusion | flops 545783808 | bytes 10765312 | tf_op jit(solution)/shard_map/while/body/eval_jaxpr/dot_general | solution.py:21
  135.3 1.5 fusion.72
  136.9 2.5 %fusion.73 = f32[2048]{0:T(1024)S(1)} fusion(f32[1024,2048]{1,0:T(8,128)S(1)} %get-tuple-element.206, f32[2048]{0:T(1024)S(1)} %max.19, pred[1024]{0:T(1024)(128)(4,1)S(1)} %dynamic-slice_reduce_fusion.2), kind=kLoop, calls=%fused_computation.22.clone.1 | loop fusion | flops 8386560 | bytes 8406016 | tf_op jit(solution)/shard_map/while/body/eval_jaxpr/reduce_sum | solution.py:20
  139.4 2.5 %fusion.74 = f32[2048,128]{1,0:T(8,128)S(1)} fusion(f32[1024,2048]{1,0:T(8,128)S(1)} %get-tuple-element.206, f32[2048]{0:T(1024)S(1)} %max.19, pred[1024]{0:T(1024)(128)(4,1)S(1)} %dynamic-slice_reduce_fusion.2, f32[2048,128]{1,0:T(8,128)S(1)} %copy-done.1, f32[2048]{0:T(1024)S(1)} %get-tuple-element.208, ...), kind=kOutput, calls=%fused_computation.25.clone.1 | convolution fusion | flops 545783808 | bytes 10765312 | tf_op jit(solution)/shard_map/while/body/eval_jaxpr/dot_general | solution.py:21
  144.0 1.6 fusion.72
  145.6 2.5 %fusion.73 = f32[2048]{0:T(1024)S(1)} fusion(f32[1024,2048]{1,0:T(8,128)S(1)} %get-tuple-element.206, f32[2048]{0:T(1024)S(1)} %max.19, pred[1024]{0:T(1024)(128)(4,1)S(1)} %dynamic-slice_reduce_fusion.2), kind=kLoop, calls=%fused_computation.22.clone.1 | loop fusion | flops 8386560 | bytes 8406016 | tf_op jit(solution)/shard_map/while/body/eval_jaxpr/reduce_sum | solution.py:20
  148.1 2.5 %fusion.74 = f32[2048,128]{1,0:T(8,128)S(1)} fusion(f32[1024,2048]{1,0:T(8,128)S(1)} %get-tuple-element.206, f32[2048]{0:T(1024)S(1)} %max.19, pred[1024]{0:T(1024)(128)(4,1)S(1)} %dynamic-slice_reduce_fusion.2, f32[2048,128]{1,0:T(8,128)S(1)} %copy-done.1, f32[2048]{0:T(1024)S(1)} %get-tuple-element.208, ...), kind=kOutput, calls=%fused_computation.25.clone.1 | convolution fusion | flops 545783808 | bytes 10765312 | tf_op jit(solution)/shard_map/while/body/eval_jaxpr/dot_general | solution.py:21
  152.7 1.5 fusion.72
  154.2 2.5 %fusion.73 = f32[2048]{0:T(1024)S(1)} fusion(f32[1024,2048]{1,0:T(8,128)S(1)} %get-tuple-element.206, f32[2048]{0:T(1024)S(1)} %max.19, pred[1024]{0:T(1024)(128)(4,1)S(1)} %dynamic-slice_reduce_fusion.2), kind=kLoop, calls=%fused_computation.22.clone.1 | loop fusion | flops 8386560 | bytes 8406016 | tf_op jit(solution)/shard_map/while/body/eval_jaxpr/reduce_sum | solution.py:20
  156.7 2.5 %fusion.74 = f32[2048,128]{1,0:T(8,128)S(1)} fusion(f32[1024,2048]{1,0:T(8,128)S(1)} %get-tuple-element.206, f32[2048]{0:T(1024)S(1)} %max.19, pred[1024]{0:T(1024)(128)(4,1)S(1)} %dynamic-slice_reduce_fusion.2, f32[2048,128]{1,0:T(8,128)S(1)} %copy-done.1, f32[2048]{0:T(1024)S(1)} %get-tuple-element.208, ...), kind=kOutput, calls=%fused_computation.25.clone.1 | convolution fusion | flops 545783808 | bytes 10765312 | tf_op jit(solution)/shard_map/while/body/eval_jaxpr/dot_general | solution.py:21
  160.2 14.0 %all-to-all-done.3 = bf16[32,128,256]{2,1,0:T(8,128)(2,1)} async-done(((bf16[32,128,256]{2,1,0:T(8,128)(2,1)}), bf16[32,128,256]{2,1,0:T(8,128)(2,1)}, u32[]{:S(2)}, u32[]{:S(2)}) %all-to-all-start.3) | async-done | bytes 2097184 | tf_op jit(solution)/shard_map/all_to_all | solution.py:85
  174.2 27.1 %while.29 = (s32[]{:T(128)}, f32[2048]{0:T(1024)S(1)}, f32[2048]{0:T(1024)S(1)}, f32[2048,128]{1,0:T(8,128)}, bf16[4,1024,256]{2,1,0:T(8,128)(2,1)}, /*index=5*/bf16[2048,128]{1,0:T(8,128)(2,1)S(1)}, s32[]{:T(128)}) while((s32[]{:T(128)}, f32[2048]{0:T(1024)S(1)}, f32[2048]{0:T(1024)S(1)}, f32[2048,128]{1,0:T(8,128)}, ...), condition=%wide.region_13.14_spmd, body=%wide.region_10.13_spmd.sunk | while | flops 1091047424 | bytes 37879944 | solution.py:39
  176.6 1.4 fusion.78
  178.0 2.0 fusion.79
  184.8 2.0 fusion.79
  190.1 1.4 fusion.78
  191.6 2.0 fusion.79
  198.4 2.0 fusion.79
  201.3 1.6 divide_convert_fusion
  (116 shorter events, 31.3 us)
Async XLA Ops:
  0.0 19.7 %copy-start = (bf16[32,128,256]{2,1,0:T(8,128)(2,1)S(1)}, bf16[32,128,256]{2,1,0:T(8,128)(2,1)}, u32[]{:S(2)}) copy-start(bf16[32,128,256]{2,1,0:T(8,128)(2,1)} %param.22) | copy-start | bytes 6291460
  0.0 19.5 %copy-start.8 = (s32[1,32]{1,0:T(1,128)S(1)}, s32[1,32]{1,0:T(1,128)}, u32[]{:S(2)}) copy-start(s32[1,32]{1,0:T(1,128)} %param.23) | copy-start | bytes 388
  0.0 19.5 %copy-start.9 = (s32[1,32]{1,0:T(1,128)S(1)}, s32[1,32]{1,0:T(1,128)}, u32[]{:S(2)}) copy-start(s32[1,32]{1,0:T(1,128)} %param.24) | copy-start | bytes 388
  16.0 52.3 %all-to-all-start.2 = ((bf16[32,128,256]{2,1,0:T(8,128)(2,1)}), bf16[32,128,256]{2,1,0:T(8,128)(2,1)}, u32[]{:S(2)}, u32[]{:S(2)}) async-start(bf16[32,128,256]{2,1,0:T(8,128)(2,1)} %bitcast.36), calls=%async_computation.2 | async-start | bytes 4194304 | tf_op jit(solution)/shard_map/all_to_all | solution.py:82
  19.7 52.7 %copy-start.5 = (bf16[256,1024]{1,0:T(8,128)(2,1)S(1)}, bf16[256,1024]{1,0:T(8,128)(2,1)}, u32[]{:S(2)}) copy-start(bf16[256,1024]{1,0:T(8,128)(2,1)} %param.15) | copy-start | bytes 1572868
  19.7 53.7 %copy-start.7 = (bf16[256,256]{1,0:T(8,128)(2,1)S(1)}, bf16[256,256]{1,0:T(8,128)(2,1)}, u32[]{:S(2)}) copy-start(bf16[256,256]{1,0:T(8,128)(2,1)} %param.16) | copy-start | bytes 393220
  21.8 52.1 %copy-start.6 = (bf16[512,256]{1,0:T(8,128)(2,1)S(1)}, bf16[512,256]{1,0:T(8,128)(2,1)}, u32[]{:S(2)}) copy-start(bf16[512,256]{1,0:T(8,128)(2,1)} %param.17) | copy-start | bytes 786436
  68.3 52.8 %all-to-all-start.1 = ((bf16[32,128,256]{2,1,0:T(8,128)(2,1)}), bf16[32,128,256]{2,1,0:T(8,128)(2,1)}, u32[]{:S(2)}, u32[]{:S(2)}) async-start(bf16[32,128,256]{2,1,0:T(8,128)(2,1)} %gather_fusion), calls=%async_computation.1 | async-start | bytes 4194304 | tf_op jit(solution)/shard_map/all_to_all | solution.py:78
  72.7 1.9 copy-start.10
  72.7 2.0 copy-start.11
  121.1 53.1 %all-to-all-start.3 = ((bf16[32,128,256]{2,1,0:T(8,128)(2,1)}), bf16[32,128,256]{2,1,0:T(8,128)(2,1)}, u32[]{:S(2)}, u32[]{:S(2)}) async-start(bf16[32,128,256]{2,1,0:T(8,128)(2,1)} %gather_fusion.2), calls=%async_computation.3 | async-start | bytes 4194304 | tf_op jit(solution)/shard_map/all_to_all | solution.py:85
  128.2 2.5 %copy-start.1 = (f32[2048,128]{1,0:T(8,128)S(1)}, f32[2048,128]{1,0:T(8,128)}, u32[]{:S(2)}) copy-start(f32[2048,128]{1,0:T(8,128)} %get-tuple-element.230) | copy-start | bytes 3145732 | tf_op jit(solution)/shard_map/while
  133.2 1.0 copy-start.2
  136.9 2.5 %copy-start.1 = (f32[2048,128]{1,0:T(8,128)S(1)}, f32[2048,128]{1,0:T(8,128)}, u32[]{:S(2)}) copy-start(f32[2048,128]{1,0:T(8,128)} %get-tuple-element.230) | copy-start | bytes 3145732 | tf_op jit(solution)/shard_map/while
  141.9 1.0 copy-start.2
  145.6 2.5 %copy-start.1 = (f32[2048,128]{1,0:T(8,128)S(1)}, f32[2048,128]{1,0:T(8,128)}, u32[]{:S(2)}) copy-start(f32[2048,128]{1,0:T(8,128)} %get-tuple-element.230) | copy-start | bytes 3145732 | tf_op jit(solution)/shard_map/while
  150.5 1.0 copy-start.2
  154.2 2.5 %copy-start.1 = (f32[2048,128]{1,0:T(8,128)S(1)}, f32[2048,128]{1,0:T(8,128)}, u32[]{:S(2)}) copy-start(f32[2048,128]{1,0:T(8,128)} %get-tuple-element.230) | copy-start | bytes 3145732 | tf_op jit(solution)/shard_map/while
  159.2 1.0 copy-start.2
  176.6 1.4 copy-start.3
  180.0 1.0 copy-start.4
  183.3 1.4 copy-start.3
  186.8 1.0 copy-start.4
  190.1 1.4 copy-start.3
  193.5 1.0 copy-start.4
  196.9 1.4 copy-start.3
  200.3 1.0 copy-start.4
where the time goes:
time: 205 us; the launch traced here: 204 us
  waiting for transfers between devices  97.5 us (48%)
  matrix products  33.3 us (16%)
  local copies, waits for them, and re-layouts  24.5 us (12%)
  other arithmetic  20 us (10%)
  blocking collectives  14.3 us (7%)
  starting transfers between devices  12 us (6%)
    all_to_all x1, waiting for transfers between devices, on_device(): lax.all_to_all(pieces, 'replica', split_axis=0, concat_axis=0, tiled=True)  46.6 us
    all_to_all x1, waiting for transfers between devices, on_device(): lax.all_to_all(outgoing, 'replica', split_axis=0, concat_axis=0, tiled=True)  37 us
    dot_general x10, matrix products, fold_block(): jnp.dot(weights.astype(jnp.bfloat16), key_value[:, head_size:], preferred...  20.9 us
    reduce_sum x10, other arithmetic, fold_block(): denominator = denominator * shrink + jnp.sum(weights, axis=1)  16.7 us
    all_to_all x1, blocking collectives, on_device(): lax.all_to_all(slot_flags, 'replica', split_axis=0, concat_axis=0, tiled=...  14.3 us
    all_to_all x1, waiting for transfers between devices, on_device(): lax.all_to_all(outgoing_pieces, 'replica', split_axis=0, concat_axis=0, t...  14 us
    dot_general x10, matrix products, fold_block(): lax.dot_general(query_rows, key_value[:, :head_size], (((1,), (1,)), ((),...  12.4 us
    squeeze x8, local copies, waits for them, and re-layouts, fold_keys(): carried, unused = lax.scan(step_block, carried, (blocks, mask_rows))  8.62 us
  transfers between devices with their start and end apart: 3, of which 3 were waited for; matrix products, arithmetic and copies ran while one was open for 21% of the time, Pallas kernels for 0%

commit v1 on v0

v1 whole, which is shorter than its diff:
```python
import functools
import math

import jax
import jax.numpy as jnp
from jax import lax
from jax.experimental import pallas as pl
from jax.experimental.pallas import tpu as pltpu
from jax.sharding import PartitionSpec as P

DEAD = 64.0
LIMIT = 32.0
MESH = pl.DeviceIdType.MESH


def attention_kernel(
    cfg,
    meta_ref,
    q_ref,
    suffix_ref,
    own_ref,
    prefix_ref,
    out_blocks,
    o_ref,
    gathered,
    first_recv,
    later_recv,
    arrived,
    m_ref,
    l_ref,
    acc_ref,
    rs_send,
    rs_recv,
    ag_send,
    ag_recv,
    st_send,
    st_recv,
    mv_send,
    mv_recv,
    local_sem,
    ready,
):
    replicas, prefixes, heads, hd = cfg
    steps = replicas.bit_length() - 1
    prefix_len = prefix_ref.shape[0]
    parts = 2
    part_rows = prefix_len // parts
    piece = part_rows // replicas
    dynamic = prefixes - 1
    orders = [list(range(steps)), list(range(steps))]
    if steps > 2:
        orders[1][1], orders[1][2] = orders[1][2], orders[1][1]
    me = lax.axis_index("replica")
    coef = hd ** (-0.5) * math.log2(math.e)

    def bit_of(device, b):
        return lax.rem(device // (1 << b), 2)

    def partner(b):
        return me + (1 - 2 * bit_of(me, b)) * (1 << b)

    def range_low(device, part, level):
        low = part * part_rows
        for t in range(level):
            low = low + bit_of(device, orders[part][t]) * (part_rows >> (t + 1))
        return low

    def rows_at(low, count):
        return pl.ds(pl.multiple_of(low, piece), count)

    barrier = pltpu.get_barrier_semaphore()

    def greet(i, c):
        pl.semaphore_signal(
            barrier, inc=1, device_id={"replica": lax.rem(me + i, replicas)}, device_id_type=MESH
        )
        return c

    lax.fori_loop(1, replicas, greet, 0)
    pl.semaphore_wait(barrier, replicas - 1)

    def rs_copy(t, part):
        b = orders[part][t]
        rows = part_rows >> (t + 1)
        low = range_low(me, part, t) + (1 - bit_of(me, b)) * rows
        if t == 0:
            src = prefix_ref.at[rows_at(low, rows), :]
            dst = first_recv.at[part]
        else:
            src = gathered.at[pl.ds(0, dynamic), rows_at(low, rows), :]
            dst = later_recv.at[part, :, pl.ds((part_rows >> 1) - 2 * rows, rows), :]
        return pltpu.make_async_remote_copy(
            src_ref=src,
            dst_ref=dst,
            send_sem=rs_send.at[t, part],
            recv_sem=rs_recv.at[t, part],
            device_id={"replica": partner(b)},
            device_id_type=MESH,
        )

    def rs_take(t, part):
        b = orders[part][t]
        rows = part_rows >> (t + 1)
        low = range_low(me, part, t) + bit_of(me, b) * rows
        for d in range(dynamic):
            other = bit_of(meta_ref[d], b) != bit_of(me, b)
            if t == 0:
                mine = prefix_ref[rows_at(low, rows), :]
                theirs = first_recv[part]
            else:
                mine = gathered[d, rows_at(low, rows), :]
                theirs = later_recv[part, d, pl.ds((part_rows >> 1) - 2 * rows, rows), :]
            gathered[d, rows_at(low, rows), :] = jnp.where(other, theirs, mine)

    def ag_copy(t, part):
        b = orders[part][t]
        rows = part_rows >> (t + 1)
        view = gathered.at[:, rows_at(range_low(me, part, t + 1), rows), :]
        return pltpu.make_async_remote_copy(
            src_ref=view,
            dst_ref=view,
            send_sem=ag_send.at[t, part],
            recv_sem=ag_recv.at[t, part],
            device_id={"replica": partner(b)},
            device_id_type=MESH,
        )

    def ag_start(t, part):
        if t > 0:
            pl.semaphore_wait(ready.at[t, part], 1)
        ag_copy(t, part).start()

    def scatter_copy(target, part):
        low = range_low(target, part, steps)
        return pltpu.make_async_remote_copy(
            src_ref=prefix_ref.at[rows_at(low, piece), :],
            dst_ref=gathered.at[prefixes - 1, rows_at(low, piece), :],
            send_sem=st_send.at[target, part],
            recv_sem=st_recv.at[part],
            device_id={"replica": target},
            device_id_type=MESH,
        )

    def move_copy(k):
        odd = lax.rem(k, 2)
        offset = odd * ((k + 1) // 2) + (1 - odd) * (replicas - k // 2)
        target = lax.rem(me + offset, replicas)
        return pltpu.make_async_remote_copy(
            src_ref=out_blocks.at[target],
            dst_ref=arrived.at[k],
            send_sem=mv_send.at[k],
            recv_sem=mv_recv.at[k],
            device_id={"replica": target},
            device_id_type=MESH,
        )

    for part in range(parts):
        rs_copy(0, part).start()

    @pl.when(me == replicas - 1)
    def _():
        def send(target, c):
            for part in range(parts):
                scatter_copy(target, part).start()
            return c

        lax.fori_loop(0, replicas - 1, send, 0)
        for part in range(parts):
            low = range_low(me, part, steps)
            gathered[prefixes - 1, rows_at(low, piece), :] = prefix_ref[rows_at(low, piece), :]

    def send_block(k, c):
        move_copy(k).start()
        return c

    lax.fori_loop(1, replicas, send_block, 0)
    local = pltpu.make_async_copy(out_blocks.at[me], arrived.at[0], local_sem)
    local.start()

    m_ref[...] = jnp.full_like(m_ref, -jnp.inf)
    l_ref[...] = jnp.zeros_like(l_ref)
    acc_ref[...] = jnp.zeros_like(acc_ref)

    def attend(load, mask_of=None):
        key_value = load()
        count = key_value.shape[0]
        mask = None if mask_of is None else mask_of()

        def one_head(h, c):
            q = q_ref[:, pl.ds(pl.multiple_of(h * hd, hd), hd)]
            scores = lax.dot_general(
                q, key_value[:, :hd], (((1,), (1,)), ((), ())), preferred_element_type=jnp.float32
            )
            if mask is not None:
                scores = jnp.where(mask, scores, -jnp.inf)
            before = m_ref[h]
            new_max = jnp.maximum(before, jnp.max(scores, axis=1, keepdims=True))
            shrink = jnp.exp2((before - new_max) * coef)
            total = l_ref[h] * shrink
            top = new_max * coef
            weights = []
            for g in range(count // hd):
                w = jnp.exp2(scores[:, g * hd : (g + 1) * hd] * coef - top)
                total = total + w
                weights.append(w.astype(jnp.bfloat16))
            l_ref[h] = total
            m_ref[h] = new_max
            acc_ref[h] = acc_ref[h] * shrink + jnp.dot(
                jnp.concatenate(weights, axis=1),
                key_value[:, hd:],
                preferred_element_type=jnp.float32,
            )
            return c

        lax.fori_loop(0, heads, one_head, 0, unroll=2)

    def attend_suffix():
        n = suffix_ref.shape[0]
        causal = lambda: (
            lax.broadcasted_iota(jnp.int32, (n, n), 1) <= lax.broadcasted_iota(jnp.int32, (n, n), 0)
        )
        attend(lambda: suffix_ref[...], causal)

    def attend_own():
        n = own_ref.shape[0]
        attend(
            lambda: own_ref[...],
            lambda: lax.broadcasted_iota(jnp.int32, (1, n), 1) < meta_ref[dynamic],
        )

    block = arrived.shape[1]
    chunk = 8

    def attend_moved(first):
        for k in range(first, first + chunk):
            if k == 0:
                local.wait()
            else:
                move_copy(k).wait_recv()
        attend(
            lambda: arrived[pl.ds(first, chunk)].reshape(chunk * block, 2 * hd),
            lambda: jnp.concatenate(
                [
                    jnp.concatenate(
                        [arrived[k, 0:16, 0:hd].astype(jnp.float32)[0:1]] * (block // hd), axis=1
                    )
                    for k in range(first, first + chunk)
                ],
                axis=1,
            )
            < LIMIT,
        )

    slot = meta_ref[dynamic + 1]

    def attend_prefix(low, rows):
        def load():
            key_value = gathered[0, rows_at(low, rows), :]
            for p in range(1, prefixes):
                key_value = jnp.where(slot == p, gathered[p, rows_at(low, rows), :], key_value)
            return key_value

        attend(load)

    for t in range(steps):
        if t == 0:
            attend_suffix()
        if t == 1:
            attend_own()
        for part in range(parts):
            rs_copy(t, part).wait()
            if t > 0:
                pl.semaphore_signal(
                    ready.at[t, part],
                    inc=1,
                    device_id={"replica": partner(orders[part][t])},
                    device_id_type=MESH,
                )
            rs_take(t, part)
            if t + 1 < steps:
                rs_copy(t + 1, part).start()

    @pl.when(me != replicas - 1)
    def _():
        for part in range(parts):
            scatter_copy(me, part).wait_recv()

    moved_groups = list(range(0, replicas, chunk))
    for part in range(parts):
        ag_start(steps - 1, part)
    for t in range(steps - 1, 0, -1):
        if t < 3 and len(moved_groups) > 2:
            attend_moved(moved_groups.pop(0))
        for part in range(parts):
            ag_copy(t, part).wait()
            ag_start(t - 1, part)
    for part in range(parts):
        attend_prefix(range_low(me, part, 1), part_rows // 2)
    while len(moved_groups) > 1:
        attend_moved(moved_groups.pop(0))
    for part in range(parts):
        ag_copy(0, part).wait()
        other = part * part_rows + (1 - bit_of(me, orders[part][0])) * (part_rows // 2)
        attend_prefix(other, part_rows // 2)
    while moved_groups:
        attend_moved(moved_groups.pop(0))

    for h in range(heads):
        denominator = jnp.sum(l_ref[h], axis=1, keepdims=True)
        o_ref[:, h * hd : (h + 1) * hd] = (acc_ref[h] / denominator).astype(o_ref.dtype)

    def sent(k, c):
        move_copy(k).wait_send()
        return c

    lax.fori_loop(1, replicas, sent, 0)

    @pl.when(me == replicas - 1)
    def _():
        def done(target, c):
            for part in range(parts):
                scatter_copy(target, part).wait_send()
            return c

        lax.fori_loop(0, replicas - 1, done, 0)


def on_device(
    queries,
    suffix_kv,
    own_cache,
    ctx_len,
    prefix_cache,
    owners,
    readers,
    kv_pool,
    mig_target,
    mig_block,
    mig_count,
):
    replicas = lax.axis_size("replica")
    me = lax.axis_index("replica")
    hd = suffix_kv.shape[1] // 2
    heads = queries.shape[1] // hd
    tokens = queries.shape[0]
    prefixes = owners.shape[0]
    targets = mig_target[0]
    block_ids = mig_block[0]
    entry_live = jnp.arange(targets.shape[0], dtype=jnp.int32) < mig_count[0]
    matching = (targets[None, :] == jnp.arange(replicas, dtype=jnp.int32)[:, None]) & entry_live[
        None, :
    ]
    slot_ids = jnp.sum(jnp.where(matching, block_ids[None, :], 0), axis=1)
    live = jnp.any(matching, axis=1)
    outgoing = jnp.where(live[:, None, None], kv_pool[slot_ids], jnp.bfloat16(DEAD))

    is_last = owners == replicas - 1
    last_at = jnp.sum(jnp.where(is_last, jnp.arange(prefixes, dtype=jnp.int32), 0))
    index = jnp.arange(prefixes - 1, dtype=jnp.int32)
    source = index + (index >= last_at)
    dynamic_owners = jnp.sum(
        jnp.where(
            source[:, None] == jnp.arange(prefixes, dtype=jnp.int32)[None, :], owners[None, :], 0
        ),
        axis=1,
    )
    mine = jnp.sum(jnp.where(jnp.arange(replicas, dtype=jnp.int32) == me, readers, 0))
    slot = jnp.where(mine == last_at, prefixes - 1, mine - (mine > last_at))
    meta = jnp.concatenate([dynamic_owners, ctx_len, slot[None]]).astype(jnp.int32)

    steps = replicas.bit_length() - 1
    prefix_len, width = prefix_cache.shape
    part_rows = prefix_len // 2
    vmem = pl.BlockSpec(memory_space=pltpu.VMEM)
    dma = pltpu.SemaphoreType.DMA
    return pl.pallas_call(
        functools.partial(attention_kernel, (replicas, prefixes, heads, hd)),
        out_shape=jax.ShapeDtypeStruct(queries.shape, jnp.bfloat16),
        in_specs=[
            pl.BlockSpec(memory_space=pltpu.SMEM),
            vmem,
            vmem,
            vmem,
            vmem,
            pl.BlockSpec(memory_space=pl.ANY),
        ],
        out_specs=vmem,
        scratch_shapes=[
            pltpu.VMEM((prefixes, prefix_len, width), jnp.bfloat16),
            pltpu.VMEM((2, part_rows // 2, width), jnp.bfloat16),
            pltpu.VMEM((2, prefixes - 1, part_rows // 2, width), jnp.bfloat16),
            pltpu.VMEM((replicas,) + kv_pool.shape[1:], jnp.bfloat16),
            pltpu.VMEM((heads, tokens, hd), jnp.float32),
            pltpu.VMEM((heads, tokens, hd), jnp.float32),
            pltpu.VMEM((heads, tokens, hd), jnp.float32),
            dma((steps, 2)),
            dma((steps, 2)),
            dma((steps, 2)),
            dma((steps, 2)),
            dma((replicas, 2)),
            dma((2,)),
            dma((replicas,)),
            dma((replicas,)),
            dma,
            pltpu.SemaphoreType.REGULAR((steps, 2)),
        ],
        compiler_params=pltpu.CompilerParams(
            collective_id=0, has_side_effects=True, vmem_limit_bytes=56 * 1024 * 1024
        ),
    )(meta, queries, suffix_kv, own_cache, prefix_cache, outgoing)


def solution(mesh):
    in_specs = (
        P(("groups", "replica"), None),
        P(("groups", "replica"), None),
        P(("groups", "replica"), None),
        P(("groups", "replica")),
        P(("groups", "replica"), None),
        P("groups"),
        P("groups"),
        P(("groups", "replica"), None, None),
        P(("groups", "replica"), None),
        P(("groups", "replica"), None),
        P(("groups", "replica")),
    )
    out_specs = P(("groups", "replica"), None)
    return jax.shard_map(
        on_device, mesh=mesh, in_specs=in_specs, out_specs=out_specs, check_vma=False
    )
```

time: 205 us -> 149 us (0.73)
  Pallas kernels: 0 us -> 130 us
  waiting for transfers between devices: 97.5 us -> 0 us
  matrix products: 33.3 us -> 0 us
  local copies, waits for them, and re-layouts: 24.5 us -> 3.91 us
  blocking collectives: 14.3 us -> 0 us
  starting transfers between devices: 12 us -> 0 us
  other arithmetic: 20 us -> 10 us
  between operations: 1.73 us -> 5.12 us
    pallas_call x0 -> x1, Pallas kernels: none -> 130 us  [on_device(): pl.pallas_call(functools.partial(attention_kernel, (replicas, prefixes, h...]
    all_to_all x3 -> x0, waiting for transfers between devices: 97.5 us -> none  [the longest x1 46.6 us: on_device(): lax.all_to_all(pieces, 'replica', split_axis=0, concat_axis=0, tiled=True)]
    dot_general x20 -> x0, matrix products: 33.3 us -> none  [the longest x10 20.9 us: fold_block(): jnp.dot(weights.astype(jnp.bfloat16), key_value[:, head_size:], preferred...]
    all_to_all x1 -> x0, blocking collectives: 14.3 us -> none  [on_device(): lax.all_to_all(slot_flags, 'replica', split_axis=0, concat_axis=0, tiled=...]
    reduce_sum x10 -> x3, other arithmetic: 16.7 us -> 3.95 us  [the longest x1 1.37 us: on_device(): jnp.sum(jnp.where(source[:, None] == jnp.arange(prefixes, dtype=jnp.int32...]
    all_to_all x3 -> x0, starting transfers between devices: 12 us -> none  [the longest x1 4.4 us: on_device(): lax.all_to_all(outgoing_pieces, 'replica', split_axis=0, concat_axis=0, t...]
    squeeze x8 -> x0, local copies, waits for them, and re-layouts: 8.62 us -> none  [fold_keys(): carried, unused = lax.scan(step_block, carried, (blocks, mask_rows))]
    while x40 -> x0, local copies, waits for them, and re-layouts: 8.03 us -> none
  transfers between devices with their start and end apart: 3 -> 0, of which waited for: 3 -> 0; matrix products, arithmetic and copies ran while one was open for 21% -> 0% of each run, Pallas kernels for 0% -> 0%
where the time goes in v1:
time: 149 us
  Pallas kernels  130 us (87%)
  other arithmetic  10 us (7%)
  between operations  5.12 us (3%)
  local copies, waits for them, and re-layouts  3.91 us (3%)
    pallas_call x1, Pallas kernels, on_device(): pl.pallas_call(functools.partial(attention_kernel, (replicas, prefixes, h...  130 us
    select_n x1, other arithmetic, on_device(): jnp.where(live[:, None, None], kv_pool[slot_ids], jnp.bfloat16(DEAD))  3.19 us

profile of v1, /device:TPU:0, one launch (start us, length us, event | category | flops | bytes accessed | tf_op | source)
XLA Modules:
  0.0 148.7 jit_solution(10675825775759571944)
XLA Ops:
  0.0 0.0 copy-start
  1.5 1.3 fusion.2
  3.3 1.4 fusion.3
  4.7 1.3 fusion.4
  9.0 1.3 pad_add_fusion.meta_ref
  10.3 0.8 select_reduce_fusion
  11.1 0.8 fusion.1
  11.9 0.0 copy-done
  11.9 2.0 %gather_fusion = bf16[32,128,256]{2,1,0:T(8,128)(2,1)} fusion(bf16[32,128,256]{2,1,0:T(8,128)(2,1)S(1)} %copy-done, s32[1024]{0:T(1024)S(1)} %pad_clamp_fusion), kind=kCustom, calls=%fused_computation | custom fusion | bytes 4194432 | tf_op jit(solution)/shard_map/gather | solution.py:355
  14.0 3.2 %broadcast_select_fusion.out_blocks = bf16[32,128,256]{2,1,0:T(8,128)(2,1)} fusion(bf16[32,128,256]{2,1,0:T(8,128)(2,1)} %gather_fusion, pred[32]{0:T(512)(128)(4,1)S(1)} %fusion.1), kind=kLoop, calls=%fused_computation.1 | loop fusion | flops 1048576 | bytes 4194336 | tf_op jit(solution)/shard_map/jit(_where)/select_n | solution.py:355
  17.2 129.7 %shard_map.109 = bf16[256,1024]{1,0:T(8,128)(2,1)} custom-call(s32[3]{0:T(128)} %pad_add_fusion.meta_ref, bf16[256,1024]{1,0:T(8,128)(2,1)} %q_ref.1, bf16[256,256]{1,0:T(8,128)(2,1)} %suffix_ref.1, bf16[512,256]{1,0:T(8,128)(2,1)} %own_ref.1, bf16[4096,256]{1,0:T(8,128)(2,1)} %prefix_ref.1, bf16[32,128,256]{2,1,0:T(8,128)(2,1)} %broadcast_select_fusion.out_blocks), custom_call_target="tpu_custom_call" | custom-call | tf_op jit(solution)/shard_map/pallas_call | solution.py:376
  146.8 1.9 %copy.15 = bf16[256,1024]{1,0:T(8,128)(2,1)} copy(bf16[256,1024]{1,0:T(8,128)(2,1)} %shard_map.109) | data formatting | bytes 1048576
  (3 shorter events, 0.0 us)
Async XLA Ops:
  0.0 11.9 %copy-start = (bf16[32,128,256]{2,1,0:T(8,128)(2,1)S(1)}, bf16[32,128,256]{2,1,0:T(8,128)(2,1)}, u32[]{:S(2)}) copy-start(bf16[32,128,256]{2,1,0:T(8,128)(2,1)} %param.18) | copy-start | bytes 6291460

commit v2 on v1

--- a/solution.py
+++ b/solution.py
@@ -20,12 +20,13 @@
     suffix_ref,
     own_ref,
     prefix_ref,
-    out_blocks,
+    pool_ref,
     o_ref,
     gathered,
     first_recv,
     later_recv,
     arrived,
+    out_blocks,
     m_ref,
     l_ref,
     acc_ref,
@@ -37,7 +38,8 @@
     st_recv,
     mv_send,
     mv_recv,
-    local_sem,
+    core_send,
+    core_recv,
     ready,
 ):
     replicas, prefixes, heads, hd = cfg
@@ -125,6 +127,22 @@
             device_id_type=MESH,
         )
 
+    def quarter(device, part, taken):
+        b = orders[part][1]
+        side = bit_of(device, b) if taken == 0 else 1 - bit_of(device, b)
+        return range_low(device, part, 1) + side * (part_rows >> 2)
+
+    def core_copy(taken, part):
+        view = gathered.at[:, rows_at(quarter(me, part, taken), part_rows >> 2), :]
+        return pltpu.make_async_remote_copy(
+            src_ref=view,
+            dst_ref=view,
+            send_sem=core_send.at[taken, part],
+            recv_sem=core_recv.at[taken, part],
+            device_id={"replica": partner(orders[part][0])},
+            device_id_type=MESH,
+        )
+
     def ag_start(t, part):
         if t > 0:
             pl.semaphore_wait(ready.at[t, part], 1)
@@ -169,13 +187,21 @@
             low = range_low(me, part, steps)
             gathered[prefixes - 1, rows_at(low, piece), :] = prefix_ref[rows_at(low, piece), :]
 
+    def picked(target):
+        code = meta_ref[dynamic + 2 + target]
+        block = pool_ref[jnp.maximum(code, 0)]
+        return jnp.where(code >= 0, block, jnp.full_like(block, DEAD))
+
     def send_block(k, c):
+        odd = lax.rem(k, 2)
+        offset = odd * ((k + 1) // 2) + (1 - odd) * (replicas - k // 2)
+        target = lax.rem(me + offset, replicas)
+        out_blocks[target] = picked(target)
         move_copy(k).start()
         return c
 
     lax.fori_loop(1, replicas, send_block, 0)
-    local = pltpu.make_async_copy(out_blocks.at[me], arrived.at[0], local_sem)
-    local.start()
+    arrived[0] = picked(me)
 
     m_ref[...] = jnp.full_like(m_ref, -jnp.inf)
     l_ref[...] = jnp.zeros_like(l_ref)
@@ -233,9 +259,7 @@
 
     def attend_moved(first):
         for k in range(first, first + chunk):
-            if k == 0:
-                local.wait()
-            else:
+            if k > 0:
                 move_copy(k).wait_recv()
         attend(
             lambda: arrived[pl.ds(first, chunk)].reshape(chunk * block, 2 * hd),
@@ -286,22 +310,31 @@
             scatter_copy(me, part).wait_recv()
 
     moved_groups = list(range(0, replicas, chunk))
+    quarter_rows = part_rows >> 2
+    beside = partner(orders[0][0])
     for part in range(parts):
         ag_start(steps - 1, part)
-    for t in range(steps - 1, 0, -1):
-        if t < 3 and len(moved_groups) > 2:
+    for t in range(steps - 1, 1, -1):
+        if t == 2:
             attend_moved(moved_groups.pop(0))
         for part in range(parts):
             ag_copy(t, part).wait()
             ag_start(t - 1, part)
-    for part in range(parts):
-        attend_prefix(range_low(me, part, 1), part_rows // 2)
-    while len(moved_groups) > 1:
-        attend_moved(moved_groups.pop(0))
-    for part in range(parts):
-        ag_copy(0, part).wait()
-        other = part * part_rows + (1 - bit_of(me, orders[part][0])) * (part_rows // 2)
-        attend_prefix(other, part_rows // 2)
+            if t == 2:
+                core_copy(0, part).start()
+    for part in range(parts):
+        attend_prefix(quarter(me, part, 0), quarter_rows)
+    for part in range(parts):
+        core_copy(0, part).wait()
+        attend_prefix(quarter(beside, part, 0), quarter_rows)
+    for part in range(parts):
+        ag_copy(1, part).wait()
+        core_copy(1, part).start()
+    for part in range(parts):
+        attend_prefix(quarter(me, part, 1), quarter_rows)
+    for part in range(parts):
+        core_copy(1, part).wait()
+        attend_prefix(quarter(beside, part, 1), quarter_rows)
     while moved_groups:
         attend_moved(moved_groups.pop(0))
 
@@ -350,9 +383,7 @@
     matching = (targets[None, :] == jnp.arange(replicas, dtype=jnp.int32)[:, None]) & entry_live[
         None, :
     ]
-    slot_ids = jnp.sum(jnp.where(matching, block_ids[None, :], 0), axis=1)
-    live = jnp.any(matching, axis=1)
-    outgoing = jnp.where(live[:, None, None], kv_pool[slot_ids], jnp.bfloat16(DEAD))
+    codes = jnp.sum(jnp.where(matching, block_ids[None, :] + 1, 0), axis=1) - 1
 
     is_last = owners == replicas - 1
     last_at = jnp.sum(jnp.where(is_last, jnp.arange(prefixes, dtype=jnp.int32), 0))
@@ -366,7 +397,7 @@
     )
     mine = jnp.sum(jnp.where(jnp.arange(replicas, dtype=jnp.int32) == me, readers, 0))
     slot = jnp.where(mine == last_at, prefixes - 1, mine - (mine > last_at))
-    meta = jnp.concatenate([dynamic_owners, ctx_len, slot[None]]).astype(jnp.int32)
+    meta = jnp.concatenate([dynamic_owners, ctx_len, slot[None], codes]).astype(jnp.int32)
 
     steps = replicas.bit_length() - 1
     prefix_len, width = prefix_cache.shape
@@ -382,13 +413,14 @@
             vmem,
             vmem,
             vmem,
-            pl.BlockSpec(memory_space=pl.ANY),
+            vmem,
         ],
         out_specs=vmem,
         scratch_shapes=[
             pltpu.VMEM((prefixes, prefix_len, width), jnp.bfloat16),
             pltpu.VMEM((2, part_rows // 2, width), jnp.bfloat16),
             pltpu.VMEM((2, prefixes - 1, part_rows // 2, width), jnp.bfloat16),
+            pltpu.VMEM((replicas,) + kv_pool.shape[1:], jnp.bfloat16),
             pltpu.VMEM((replicas,) + kv_pool.shape[1:], jnp.bfloat16),
             pltpu.VMEM((heads, tokens, hd), jnp.float32),
             pltpu.VMEM((heads, tokens, hd), jnp.float32),
@@ -401,13 +433,14 @@
             dma((2,)),
             dma((replicas,)),
             dma((replicas,)),
-            dma,
+            dma((2, 2)),
+            dma((2, 2)),
             pltpu.SemaphoreType.REGULAR((steps, 2)),
         ],
         compiler_params=pltpu.CompilerParams(
             collective_id=0, has_side_effects=True, vmem_limit_bytes=56 * 1024 * 1024
         ),
-    )(meta, queries, suffix_kv, own_cache, prefix_cache, outgoing)
+    )(meta, queries, suffix_kv, own_cache, prefix_cache, kv_pool)
 
 
 def solution(mesh):

time: 149 us -> 144 us (0.966); the launches traced: 149 us -> 142 us
  other arithmetic: 10 us -> 6.76 us
  local copies, waits for them, and re-layouts: 3.91 us -> 1.87 us
  Pallas kernels: 130 us -> 128 us
    select_n x2 -> x0, other arithmetic: 3.2 us -> none  [the longest x1 3.19 us: on_device(): jnp.where(live[:, None, None], kv_pool[slot_ids], jnp.bfloat16(DEAD))]
    gather x1 -> x0, local copies, waits for them, and re-layouts: 2.03 us -> none  [on_device(): kv_pool[slot_ids]]
    pallas_call x1, Pallas kernels: 130 us -> 128 us  [on_device(): pl.pallas_call(functools.partial(attention_kernel, (replicas, prefixes, h...]
where the time goes in v2:
time: 144 us; the launch traced here: 142 us
  Pallas kernels  128 us (89%)
  other arithmetic  6.76 us (5%)
  between operations  4.94 us (3%)
  local copies, waits for them, and re-layouts  1.87 us (1%)
    pallas_call x1, Pallas kernels, on_device(): pl.pallas_call(functools.partial(attention_kernel, (replicas, prefixes, h...  128 us

profile of v2, /device:TPU:0, one launch (start us, length us, event | category | flops | bytes accessed | tf_op | source)
XLA Modules:
  0.0 141.6 jit_solution(2697308126394518245)
XLA Ops:
  1.3 1.3 fusion.1
  3.2 1.4 fusion.2
  4.5 1.3 fusion.3
  8.9 0.7 add_bitcast_fusion
  9.6 0.8 select_reduce_fusion
  10.3 1.4 pad_add_fusion.meta_ref
  11.7 128.0 %shard_map.109 = bf16[256,1024]{1,0:T(8,128)(2,1)} custom-call(s32[35]{0:T(128)} %pad_add_fusion.meta_ref, bf16[256,1024]{1,0:T(8,128)(2,1)} %q_ref.1, bf16[256,256]{1,0:T(8,128)(2,1)} %suffix_ref.1, bf16[512,256]{1,0:T(8,128)(2,1)} %own_ref.1, bf16[4096,256]{1,0:T(8,128)(2,1)} %prefix_ref.1, bf16[32,128,256]{2,1,0:T(8,128)(2,1)} %pool_ref.1), custom_call_target="tpu_custom_call" | custom-call | tf_op jit(solution)/shard_map/pallas_call | solution.py:407
  139.7 1.9 %copy.15 = bf16[256,1024]{1,0:T(8,128)(2,1)} copy(bf16[256,1024]{1,0:T(8,128)(2,1)} %shard_map.109) | data formatting | bytes 1048576
  (2 shorter events, 0.0 us)
